TPU v7x, 32 devices: a whole 2x2x4 slice. The times are simulated.
32 devices in a mesh: groups: 2 (over y), rows: 8 (over z, x), cols: 2 (over core).
Axes of the slice: x: 2, y: 2, z: 4, core: 2. Of those that a mesh axis runs over, the one named last changes fastest.
Arguments:
- series_a: float32 [4, 8192], P(None, ('groups', 'rows')), parts along dimension 1, may hold values from -100 to 100
- series_b: float32 [4, 2048], P(None, ('groups', 'rows', 'cols')), parts along dimension 1, may hold values from -100 to 100
- a_offsets: int32 [16], P(('groups', 'rows')), parts along dimension 0, may hold values from 0 to 511
- b_offsets: int32 [4], P(('groups', 'cols')), parts along dimension 0, may hold values from 0 to 511
Outputs:
- a_profile: float32 [8192, 16], P(('groups', 'rows', 'cols')), parts along dimension 0
- b_profile: float32 [4, 512, 16], P(('groups', 'cols'), 'rows'), parts along dimension 0
There are 2 independent parts, one for each index of `groups`. A program takes and returns all parts, laid end to end along the dimension named above; each array names one. Nothing has to cross between parts.
All inputs are finite; a program needn't handle non-finite values.
Results may differ from a plain program's by a relative error of at most 0.00046.
Values sent between devices are 32-bit elements; how exact they have to be, the bound alone decides.
A program may use at most 64 MiB of HBM per device.

v0:
```python
import functools

import jax
import jax.numpy as jnp
from jax import lax
from jax.experimental import pallas as pl
from jax.experimental.pallas import tpu as pltpu
from jax.sharding import PartitionSpec as P

M = 512
K = 16
NA = 512
NB = 512
LANES = 128
SUB = 8
SPAN = NA + M
WIDE = SPAN - LANES
MESH = pl.DeviceIdType.MESH


def comparators(n):
    pairs = []
    p = 1
    while p < n:
        k = p
        while k >= 1:
            for j in range(k % p, n - k, 2 * k):
                for i in range(min(k, n - j - k)):
                    if (i + j) // (2 * p) == (i + j + k) // (2 * p):
                        pairs.append((i + j, i + j + k))
            k //= 2
        p *= 2
    return pairs


def sort_desc(x):
    x = list(x)
    for i, j in comparators(len(x)):
        x[i], x[j] = jnp.maximum(x[i], x[j]), jnp.minimum(x[i], x[j])
    return x


def merge_top(a, b):
    n = len(a)
    x = [jnp.maximum(a[j], b[n - 1 - j]) for j in range(n)]
    d = n // 2
    while d >= 1:
        for j in range(n):
            if not j & d:
                x[j], x[j + d] = jnp.maximum(x[j], x[j + d]), jnp.minimum(x[j], x[j + d])
        d //= 2
    return x


def merge_sublanes(x):
    n = x[0].shape[0]
    while n > SUB:
        n //= 2
        x = merge_top([v[:n] for v in x], [v[n:] for v in x])
    d = n // 2
    while d >= 1:
        x = merge_top(x, [pltpu.roll(v, d, 0) for v in x])
        d //= 2
    return [v[0:1] for v in x]


def top_columns(ref, lanes):
    rows = ref.shape[0]
    lists = None
    for base in range(0, rows, K * SUB):
        group = sort_desc([ref[pl.ds(base + SUB * v, SUB), lanes] for v in range(K)])
        lists = group if lists is None else merge_top(lists, group)
    return merge_sublanes(lists)


def hankel(segment, h_ref):
    sums = []
    sub = lax.broadcasted_iota(jnp.int32, (SUB, SPAN), 0)
    for c in range(segment.shape[0]):
        t = jnp.broadcast_to(segment[c : c + 1], (SUB, SPAN))
        for bit in (1, 2, 4):
            t = jnp.where((sub & bit) != 0, pltpu.roll(t, SPAN - bit, 1), t)
        total = None
        for b in range(LANES // SUB):
            piece = t if b == 0 else pltpu.roll(t, SPAN - SUB * b, 1)
            piece = piece[:, :WIDE]
            h_ref[c, SUB * b : SUB * b + SUB, :] = piece
            total = piece if total is None else total + piece
        sums.append(jnp.sum(total, axis=0, keepdims=True))
    return sums


def unit_stats(h_ref, sums):
    found = []
    parts = range(M // LANES)
    for c in range(len(sums)):
        centre = sums[c] * (1.0 / LANES)
        about = jnp.broadcast_to(centre, (SUB, WIDE))

        def squares(b, total):
            d = h_ref[c, pl.ds(pl.multiple_of(b * SUB, SUB), SUB), :] - about
            return total + d * d

        total = lax.fori_loop(0, LANES // SUB, squares, jnp.zeros((SUB, WIDE), jnp.float32), unroll=16)
        within = jnp.sum(total, axis=0, keepdims=True)
        means = [centre[:, LANES * q : LANES * q + NA] for q in parts]
        mean = sum(means[1:], means[0]) * (LANES / M)
        spread = sum(within[:, LANES * q : LANES * q + NA] for q in parts)
        for v in means:
            spread = spread + LANES * ((v - mean) * (v - mean))
        found.append((mean, lax.rsqrt(spread * (1.0 / M) + 1e-05)))
    return found


def kernel(
    rows, cols, aoff_hbm, boff_hbm, a_hbm, b_hbm, a_out, b_out,
    aoff, boff, abuf, bbuf, ha, hb, left, right, spread_out, score, score_t, alist, blist, arecv, brecv,
    own_sem, a_send, a_recv, b_send, b_recv, la_send, la_recv, lb_send, lb_recv,
):
    channels = a_hbm.shape[0]
    count = rows * cols
    g = lax.axis_index("groups")
    r = lax.axis_index("rows")
    k = lax.axis_index("cols")
    me = r * cols + k

    def ahead(x, d, n):
        y = x + d
        return y if d == 0 else jnp.where(y >= n, y - n, y)

    along = [ahead(r, d, rows) for d in range(rows)]
    across = [ahead(k, d, cols) for d in range(cols)]
    peers = [(i, j) for i in along for j in across][1:]

    own_a = pltpu.make_async_copy(a_hbm, abuf.at[1], own_sem.at[0])
    own_b = pltpu.make_async_copy(b_hbm, bbuf.at[me], own_sem.at[1])
    offset_a = pltpu.make_async_copy(aoff_hbm, aoff, own_sem.at[2])
    offset_b = pltpu.make_async_copy(boff_hbm, boff, own_sem.at[3])
    for copy in (own_a, own_b, offset_a, offset_b):
        copy.start()

    barrier = pltpu.get_barrier_semaphore()
    for i, j in peers:
        pl.semaphore_signal(barrier, inc=1, device_id=(g, i, j), device_id_type=MESH)
    pl.semaphore_wait(barrier, count - 1)

    after = along[1]
    before = along[rows - 1]
    a_copies = [
        pltpu.make_async_remote_copy(
            src_ref=a_hbm, dst_ref=abuf.at[slot], send_sem=a_send.at[slot], recv_sem=a_recv.at[slot],
            device_id=(g, to, k), device_id_type=MESH,
        )
        for slot, to in ((0, after), (2, before))
    ]
    for copy in a_copies:
        copy.start()
    b_copies = []
    for d, (i, j) in enumerate(peers):
        b_copies.append(
            pltpu.make_async_remote_copy(
                src_ref=b_hbm, dst_ref=bbuf.at[me], send_sem=b_send.at[d], recv_sem=b_recv.at[me],
                device_id=(g, i, j), device_id_type=MESH,
            )
        )
        b_copies[-1].start()

    own_a.wait()
    offset_a.wait()
    for copy in a_copies:
        copy.wait_recv()
    padded = jnp.concatenate([abuf[0], abuf[1], abuf[2]], axis=1)
    extent = padded.shape[1]
    segment = pltpu.roll(padded, lax.rem(extent - aoff[0], extent), 1)[:, :SPAN]
    stats = unit_stats(ha, hankel(segment, ha))
    rest = jnp.concatenate([v for pair in stats for v in pair], axis=0)
    pieces = []
    for _ in range(3):
        pieces.append(rest.astype(jnp.bfloat16).astype(jnp.float32))
        rest = rest - pieces[-1]
    split = jnp.concatenate(pieces, axis=0).T.astype(jnp.bfloat16)
    kinds = 2 * channels
    shape = (3 * kinds, kinds * LANES)
    chosen = lax.broadcasted_iota(jnp.int32, shape, 0) % kinds == lax.broadcasted_iota(jnp.int32, shape, 1) // LANES
    spread_out[...] = jnp.dot(
        split, jnp.where(chosen, 1.0, 0.0).astype(jnp.bfloat16), preferred_element_type=jnp.float32
    )

    @pl.loop(0, LANES // 16, unroll=True)
    def _(b):
        at = pl.multiple_of(b * 16, 16)
        for q in range(NA // LANES):
            row = pl.multiple_of(at + LANES * q, 16)
            for c in range(channels):
                mean = spread_out[pl.ds(row, 16), 2 * c * LANES : (2 * c + 1) * LANES]
                scale = spread_out[pl.ds(row, 16), (2 * c + 1) * LANES : (2 * c + 2) * LANES]
                for m in range(0, M, LANES):
                    w = ha[c, pl.ds(at, 16), LANES * q + m : LANES * q + m + LANES]
                    left[pl.ds(row, 16), M * c + m : M * c + m + LANES] = ((w - mean) * scale).astype(jnp.bfloat16)

    own_b.wait()
    offset_b.wait()
    for d, (i, j) in enumerate(peers):
        source = i * cols + j
        pltpu.make_async_remote_copy(
            src_ref=b_hbm, dst_ref=bbuf.at[source], send_sem=b_send.at[d], recv_sem=b_recv.at[source],
            device_id=(g, i, j), device_id_type=MESH,
        ).wait_recv()
    whole = jnp.concatenate([bbuf[p] for p in range(count)], axis=1)
    extent_b = whole.shape[1]
    start = lax.rem(k * NB + boff[0], extent_b)
    segment_b = pltpu.roll(whole, lax.rem(extent_b - start, extent_b), 1)
    stats_b = unit_stats(hb, hankel(segment_b, hb))
    for c in range(channels):
        mean16 = jnp.broadcast_to(stats_b[c][0], (16, NB))
        scale16 = jnp.broadcast_to(stats_b[c][1], (16, NB))

        @pl.loop(0, LANES // 16, unroll=True)
        def _(b):
            at = pl.multiple_of(b * 16, 16)
            for q in range(M // LANES):
                w = hb[c, pl.ds(at, 16), LANES * q : LANES * q + NB]
                right[pl.ds(pl.multiple_of(at + M * c + LANES * q, 16), 16), :] = (
                    (w - mean16) * scale16
                ).astype(jnp.bfloat16)

    score[...] = jnp.dot(left[...], right[...], preferred_element_type=jnp.float32) * (1.0 / (channels * M))

    share_b = NB // rows
    per = LANES // share_b
    tiles = NB // LANES
    own = r // per
    place = r - own * per
    lb_copies = []

    def send_list(to):
        lb_copies.append(
            pltpu.make_async_remote_copy(
                src_ref=blist.at[to], dst_ref=brecv.at[r], send_sem=lb_send.at[len(lb_copies)], recv_sem=lb_recv.at[r],
                device_id=(g, to, k), device_id_type=MESH,
            )
        )
        lb_copies[-1].start()

    for n in range(tiles):
        if n == tiles - 1:
            t = own
        else:
            down = tiles - 1 - n
            t = jnp.where(
                2 * own < tiles - 1,
                jnp.where(own >= down, down - 1, down),
                jnp.where(own <= n, n + 1, n),
            )
        found = jnp.concatenate(top_columns(score, pl.ds(pl.multiple_of(LANES * t, LANES), LANES)), axis=0)
        for u in range(per):
            blist[t * per + u] = found[:, u * share_b : (u + 1) * share_b]
        for u in range(per - 1 if n == tiles - 1 else per):
            send_list(t * per + (ahead(place, u + 1, per) if n == tiles - 1 else u))
    brecv[r] = blist[r]

    score_t[...] = score[...].T
    share_a = NA // cols
    for t in range(NA // LANES):
        found = jnp.concatenate(top_columns(score_t, pl.ds(LANES * t, LANES)), axis=0)
        alist[(LANES * t) // share_a, :, (LANES * t) % share_a : (LANES * t) % share_a + LANES] = found
    la_copies = []
    for d in range(1, cols):
        to = across[d]
        la_copies.append(
            pltpu.make_async_remote_copy(
                src_ref=alist.at[to], dst_ref=arecv.at[k], send_sem=la_send.at[d], recv_sem=la_recv.at[k],
                device_id=(g, r, to), device_id_type=MESH,
            )
        )
        la_copies[-1].start()

    for d in range(1, rows):
        source = along[d]
        pltpu.make_async_remote_copy(
            src_ref=blist.at[source], dst_ref=brecv.at[source], send_sem=lb_send.at[d], recv_sem=lb_recv.at[source],
            device_id=(g, source, k), device_id_type=MESH,
        ).wait_recv()
    lists = [brecv[:, j, :] for j in range(K)]
    b_out[...] = jnp.concatenate(merge_sublanes(lists), axis=0)

    held = alist[k]
    best = [held[j : j + 1] for j in range(K)]
    for d in range(1, cols):
        source = across[d]
        pltpu.make_async_remote_copy(
            src_ref=alist.at[source], dst_ref=arecv.at[source], send_sem=la_send.at[d], recv_sem=la_recv.at[source],
            device_id=(g, r, source), device_id_type=MESH,
        ).wait_recv()
        came = arecv[source]
        best = merge_top(best, [came[j : j + 1] for j in range(K)])
    a_out[...] = jnp.concatenate(best, axis=0)

    for copy in a_copies + b_copies + lb_copies + la_copies:
        copy.wait_send()


def local(rows, cols, series_a, series_b, a_offsets, b_offsets):
    channels, length_a = series_a.shape
    length_b = series_b.shape[1]
    count = rows * cols
    share_a = NA // cols
    share_b = NB // rows
    vmem = pl.BlockSpec(memory_space=pltpu.VMEM)
    hbm = pl.BlockSpec(memory_space=pltpu.HBM)
    dma = pltpu.SemaphoreType.DMA
    f32 = jnp.float32
    a_best, b_best = pl.pallas_call(
        functools.partial(kernel, rows, cols),
        out_shape=(
            pltpu.VMEM((K, share_a), f32),
            pltpu.VMEM((K, share_b), f32),
        ),
        in_specs=[hbm] * 4,
        out_specs=(vmem, vmem),
        scratch_shapes=[
            pltpu.SMEM((1,), jnp.int32),
            pltpu.SMEM((1,), jnp.int32),
            pltpu.VMEM((3, channels, length_a), f32),
            pltpu.VMEM((count, channels, length_b), f32),
            pltpu.VMEM((channels, LANES, WIDE), f32),
            pltpu.VMEM((channels, LANES, WIDE), f32),
            pltpu.VMEM((NA, channels * M), jnp.bfloat16),
            pltpu.VMEM((channels * M, NB), jnp.bfloat16),
            pltpu.VMEM((NA, 2 * channels * LANES), f32),
            pltpu.VMEM((NA, NB), f32),
            pltpu.VMEM((NB, NA), f32),
            pltpu.VMEM((cols, K, share_a), f32),
            pltpu.VMEM((rows, K, share_b), f32),
            pltpu.VMEM((cols, K, share_a), f32),
            pltpu.VMEM((rows, K, share_b), f32),
            dma((4,)),
            dma((3,)),
            dma((3,)),
            dma((count,)),
            dma((count,)),
            dma((cols,)),
            dma((cols,)),
            dma((rows,)),
            dma((rows,)),
        ],
        compiler_params=pltpu.CompilerParams(collective_id=0, has_side_effects=True),
        name="join",
    )(a_offsets, b_offsets, series_a, series_b)
    return (a_best.T, b_best.T[None])


def solution(mesh):
    in_specs = (
        P(None, ("groups", "rows")),
        P(None, ("groups", "rows", "cols")),
        P(("groups", "rows")),
        P(("groups", "cols")),
    )
    out_specs = (P(("groups", "rows", "cols"), None), P(("groups", "cols"), "rows", None))
    body = functools.partial(local, mesh.shape["rows"], mesh.shape["cols"])
    return jax.shard_map(body, mesh=mesh, in_specs=in_specs, out_specs=out_specs, check_vma=False)
```

profile of v0, /device:TPU:0, one launch (start us, length us, event | category | flops | bytes accessed | tf_op | source)
XLA Modules:
  0.0 22.7 jit_solution(10470078063696398470)
XLA Ops:
  1.9 19.5 %join.1 = (f32[16,256]{1,0:T(8,128)S(1)}, f32[16,64]{1,0:T(8,128)S(1)}) custom-call(s32[1]{0:T(128)S(6)} %copy.10.aoff_hbm, s32[1]{0:T(128)S(6)} %copy.11.boff_hbm, f32[4,512]{1,0:T(4,128)} %a_hbm.1, f32[4,64]{1,0:T(4,128)} %b_hbm.1), custom_call_target="tpu_custom_call" | custom-call | tf_op jit(solution)/shard_map/join/pallas_call | solution.py:313
  21.5 0.6 %copy.8 = f32[256,16]{0,1:T(8,128)} copy(f32[256,16]{0,1:T(8,128)S(1)} %bitcast.4) | data formatting | bytes 32768
  22.1 0.6 %copy.9 = f32[1,64,16]{1,2,0:T(8,128)} copy(f32[1,64,16]{1,2,0:T(8,128)S(1)} %bitcast.5) | data formatting | bytes 8192
where the time goes:
time: 22.8 us; the launch traced here: 22.7 us
  Pallas kernels  19.5 us (86%)
  between operations  1.93 us (8%)
  local copies, waits for them, and re-layouts  1.21 us (5%)
    pallas_call x1, Pallas kernels, local(): pl.pallas_call(functools.partial(kernel, rows, cols), out_shape=(pltpu.VM...  19.5 us
    unnamed x2, local copies, waits for them, and re-layouts  1.21 us

commit v1 on v0

v1 whole, which is shorter than its diff:
```python
import functools

import jax
import jax.numpy as jnp
from jax import lax
from jax.experimental import pallas as pl
from jax.experimental.pallas import tpu as pltpu
from jax.sharding import PartitionSpec as P

M = 512
K = 16
NA = 512
NB = 512
LANES = 128
SUB = 8
SPAN = NA + M
WIDE = SPAN - LANES
MESH = pl.DeviceIdType.MESH


def comparators(n):
    pairs = []
    p = 1
    while p < n:
        k = p
        while k >= 1:
            for j in range(k % p, n - k, 2 * k):
                for i in range(min(k, n - j - k)):
                    if (i + j) // (2 * p) == (i + j + k) // (2 * p):
                        pairs.append((i + j, i + j + k))
            k //= 2
        p *= 2
    return pairs


def sort_desc(x):
    x = list(x)
    for i, j in comparators(len(x)):
        x[i], x[j] = jnp.maximum(x[i], x[j]), jnp.minimum(x[i], x[j])
    return x


def merge_top(a, b):
    n = len(a)
    x = [jnp.maximum(a[j], b[n - 1 - j]) for j in range(n)]
    d = n // 2
    while d >= 1:
        for j in range(n):
            if not j & d:
                x[j], x[j + d] = jnp.maximum(x[j], x[j + d]), jnp.minimum(x[j], x[j + d])
        d //= 2
    return x


def merge_sublanes(x):
    n = x[0].shape[0]
    while n > SUB:
        n //= 2
        x = merge_top([v[:n] for v in x], [v[n:] for v in x])
    d = n // 2
    while d >= 1:
        x = merge_top(x, [pltpu.roll(v, d, 0) for v in x])
        d //= 2
    return [v[0:1] for v in x]


def column_lists(ref, lanes):
    rows = ref.shape[0]
    lists = None
    for base in range(0, rows, K * SUB):
        group = sort_desc([ref[pl.ds(base + SUB * v, SUB), lanes] for v in range(K)])
        lists = group if lists is None else merge_top(lists, group)
    return lists


def hankel(segment, h_ref):
    sums = []
    sub = lax.broadcasted_iota(jnp.int32, (SUB, SPAN), 0)
    for c in range(segment.shape[0]):
        t = jnp.broadcast_to(segment[c : c + 1], (SUB, SPAN))
        for bit in (1, 2, 4):
            t = jnp.where((sub & bit) != 0, pltpu.roll(t, SPAN - bit, 1), t)
        total = None
        for b in range(LANES // SUB):
            piece = t if b == 0 else pltpu.roll(t, SPAN - SUB * b, 1)
            piece = piece[:, :WIDE]
            h_ref[c, SUB * b : SUB * b + SUB, :] = piece
            total = piece if total is None else total + piece
        sums.append(jnp.sum(total, axis=0, keepdims=True))
    return sums


def unit_stats(h_ref, sums):
    found = []
    parts = range(M // LANES)
    for c in range(len(sums)):
        centre = sums[c] * (1.0 / LANES)
        about = jnp.broadcast_to(centre, (SUB, WIDE))

        def squares(b, total):
            d = h_ref[c, pl.ds(pl.multiple_of(b * SUB, SUB), SUB), :] - about
            return total + d * d

        total = lax.fori_loop(0, LANES // SUB, squares, jnp.zeros((SUB, WIDE), jnp.float32), unroll=16)
        within = jnp.sum(total, axis=0, keepdims=True)
        means = [centre[:, LANES * q : LANES * q + NA] for q in parts]
        mean = sum(means[1:], means[0]) * (LANES / M)
        spread = sum(within[:, LANES * q : LANES * q + NA] for q in parts)
        for v in means:
            spread = spread + LANES * ((v - mean) * (v - mean))
        found.append((mean, lax.rsqrt(spread * (1.0 / M) + 1e-05)))
    return found


def normalise_rows(padded, offset, h_ref, spread_ref, left):
    channels, extent = padded.shape
    segment = pltpu.roll(padded, lax.rem(extent - offset, extent), 1)[:, :SPAN]
    stats = unit_stats(h_ref, hankel(segment, h_ref))
    rest = jnp.concatenate([v for pair in stats for v in pair], axis=0)
    pieces = []
    for _ in range(3):
        pieces.append(rest.astype(jnp.bfloat16).astype(jnp.float32))
        rest = rest - pieces[-1]
    split = jnp.concatenate(pieces, axis=0).T.astype(jnp.bfloat16)
    kinds = 2 * channels
    shape = (3 * kinds, kinds * LANES)
    chosen = lax.broadcasted_iota(jnp.int32, shape, 0) % kinds == lax.broadcasted_iota(jnp.int32, shape, 1) // LANES
    spread_ref[...] = jnp.dot(
        split, jnp.where(chosen, 1.0, 0.0).astype(jnp.bfloat16), preferred_element_type=jnp.float32
    )

    @pl.loop(0, LANES // 16, unroll=True)
    def _(b):
        at = pl.multiple_of(b * 16, 16)
        for q in range(NA // LANES):
            row = pl.multiple_of(at + LANES * q, 16)
            for c in range(channels):
                mean = spread_ref[pl.ds(row, 16), 2 * c * LANES : (2 * c + 1) * LANES]
                scale = spread_ref[pl.ds(row, 16), (2 * c + 1) * LANES : (2 * c + 2) * LANES]
                for m in range(0, M, LANES):
                    w = h_ref[c, pl.ds(at, 16), LANES * q + m : LANES * q + m + LANES]
                    left[pl.ds(row, 16), M * c + m : M * c + m + LANES] = ((w - mean) * scale).astype(jnp.bfloat16)


def shifted(x, lanes):
    lanes %= x.shape[1]
    return x if lanes == 0 else pltpu.roll(x, lanes, 1)


def kernel(
    rows, cols, aoff_hbm, boff_hbm, a_hbm, b_hbm, a_out, b_out,
    aoff, boff, off_out, off_in, abuf, bbuf, ha, hb, left, right, spread_out, score, score_far, score_t,
    alist, blist, arecv, brecv,
    own_sem, off_send, off_recv, a_send, a_recv, b_send, b_recv, la_send, la_recv, lb_send, lb_recv,
):
    channels = a_hbm.shape[0]
    count = rows * cols
    half = rows // 2
    g = lax.axis_index("groups")
    r = lax.axis_index("rows")
    k = lax.axis_index("cols")
    me = r * cols + k

    def ahead(x, d, n):
        d %= n
        y = x + d
        return y if d == 0 else jnp.where(y >= n, y - n, y)

    across = [ahead(k, d, cols) for d in range(cols)]
    if rows & (rows - 1):
        along = [ahead(r, d, rows) for d in range(rows)]
    else:
        along = [r ^ d for d in range(rows)]
    peers = [(i, j) for i in along[::-1] for j in across[::-1]][:-1]

    own_a = pltpu.make_async_copy(a_hbm, abuf.at[1], own_sem.at[0])
    own_b = pltpu.make_async_copy(b_hbm, bbuf.at[me], own_sem.at[1])
    offset_a = pltpu.make_async_copy(aoff_hbm, aoff, own_sem.at[2])
    offset_b = pltpu.make_async_copy(boff_hbm, boff, own_sem.at[3])
    for copy in (offset_a, own_a, own_b, offset_b):
        copy.start()

    barrier = pltpu.get_barrier_semaphore()
    for i, j in peers:
        pl.semaphore_signal(barrier, inc=1, device_id=(g, i, j), device_id_type=MESH)
    offset_a.wait()
    off_out[...] = jnp.full(off_out.shape, aoff[0], jnp.int32)
    pl.semaphore_wait(barrier, count - 1)

    def remote(src, dst, send, recv, to):
        return pltpu.make_async_remote_copy(
            src_ref=src, dst_ref=dst, send_sem=send, recv_sem=recv, device_id=to, device_id_type=MESH
        )

    far = ahead(r, half, rows)
    a_copies = [
        remote(a_hbm, abuf.at[slot], a_send.at[slot], a_recv.at[slot], (g, ahead(r, -d, rows), k))
        for slot, d in ((0, -1), (2, 1), (4, half), (3, half - 1), (5, half + 1))
    ]
    b_copies = [
        remote(b_hbm, bbuf.at[me], b_send.at[d], b_recv.at[me], (g, i, j)) for d, (i, j) in enumerate(peers)
    ]
    off_copy = remote(off_out, off_in, off_send.at[0], off_recv.at[0], (g, far, k))
    for copy in a_copies[:2] + b_copies + [off_copy] + a_copies[2:]:
        copy.start()

    own_a.wait()
    for copy in a_copies[:2]:
        copy.wait_recv()
    padded = jnp.concatenate([abuf[0], abuf[1], abuf[2]], axis=1)
    normalise_rows(padded, aoff[0], ha.at[0], spread_out.at[0], left.at[0])

    off_copy.wait_recv()
    for copy in a_copies[2:]:
        copy.wait_recv()
    padded = jnp.concatenate([abuf[3], abuf[4], abuf[5]], axis=1)
    normalise_rows(padded, jnp.max(off_in[...]), ha.at[1], spread_out.at[1], left.at[1])

    own_b.wait()
    offset_b.wait()
    for d, (i, j) in enumerate(peers):
        source = i * cols + j
        remote(b_hbm, bbuf.at[source], b_send.at[d], b_recv.at[source], (g, i, j)).wait_recv()
    whole = jnp.concatenate([bbuf[p] for p in range(count)], axis=1)
    extent_b = whole.shape[1]
    start = lax.rem(k * NB + boff[0], extent_b)
    segment_b = pltpu.roll(whole, lax.rem(extent_b - start, extent_b), 1)
    stats_b = unit_stats(hb, hankel(segment_b, hb))
    for c in range(channels):
        mean16 = jnp.broadcast_to(stats_b[c][0], (16, NB))
        scale16 = jnp.broadcast_to(stats_b[c][1], (16, NB))

        @pl.loop(0, LANES // 16, unroll=True)
        def _(b):
            at = pl.multiple_of(b * 16, 16)
            for q in range(M // LANES):
                w = hb[c, pl.ds(at, 16), LANES * q : LANES * q + NB]
                right[pl.ds(pl.multiple_of(at + M * c + LANES * q, 16), 16), :] = (
                    (w - mean16) * scale16
                ).astype(jnp.bfloat16)

    factor = 1.0 / (channels * M)
    score[...] = jnp.dot(left[0], right[...], preferred_element_type=jnp.float32) * factor
    reach = NB // 2
    side = r // half
    base = pl.multiple_of(side * reach, LANES)
    score_far[...] = jnp.dot(left[1], right[:, pl.ds(base, reach)], preferred_element_type=jnp.float32) * factor

    share_b = NB // rows
    per = LANES // share_b
    depth = K // per
    block = lax.broadcasted_iota(jnp.int32, (depth, LANES), 1) // share_b
    lb_copies = []
    for t in range(reach // LANES):
        near_list = column_lists(score, pl.ds(pl.multiple_of(base + LANES * t, LANES), LANES))
        far_list = column_lists(score_far, pl.ds(LANES * t, LANES))
        found = jnp.concatenate(merge_sublanes(merge_top(near_list, far_list)), axis=0)
        for u in range(per):
            packed = None
            for v in range(per):
                piece = shifted(found[depth * v : depth * v + depth], (v - u) * share_b)
                packed = piece if packed is None else jnp.where(block == v, piece, packed)
            blist[t * per + u] = packed
    low = side * half
    mine = r - low
    for d in range(1, half):
        to = mine ^ d if half & (half - 1) == 0 else ahead(mine, d, half)
        lb_copies.append(remote(blist.at[to], brecv.at[mine], lb_send.at[d], lb_recv.at[mine], (g, low + to, k)))
        lb_copies[-1].start()
    brecv[mine] = blist[mine]

    score_t[...] = score[...].T
    share_a = NA // cols
    for t in range(NA // LANES):
        found = jnp.concatenate(merge_sublanes(column_lists(score_t, pl.ds(LANES * t, LANES))), axis=0)
        alist[(LANES * t) // share_a, :, (LANES * t) % share_a : (LANES * t) % share_a + LANES] = found
    la_copies = []
    for d in range(1, cols):
        to = across[d]
        la_copies.append(remote(alist.at[to], arecv.at[k], la_send.at[d], la_recv.at[k], (g, r, to)))
        la_copies[-1].start()

    for d in range(1, half):
        source = mine ^ d if half & (half - 1) == 0 else ahead(mine, d, half)
        remote(blist.at[source], brecv.at[source], lb_send.at[d], lb_recv.at[source], (g, low + source, k)).wait_recv()
    lists = [brecv[:, j % depth, (j // depth) * share_b : (j // depth + 1) * share_b] for j in range(K)]
    b_out[...] = jnp.concatenate(merge_sublanes(lists), axis=0)

    held = alist[k]
    best = [held[j : j + 1] for j in range(K)]
    for d in range(1, cols):
        source = across[d]
        remote(alist.at[source], arecv.at[source], la_send.at[d], la_recv.at[source], (g, r, source)).wait_recv()
        came = arecv[source]
        best = merge_top(best, [came[j : j + 1] for j in range(K)])
    a_out[...] = jnp.concatenate(best, axis=0)

    for copy in a_copies + b_copies + [off_copy] + lb_copies + la_copies:
        copy.wait_send()


def local(rows, cols, series_a, series_b, a_offsets, b_offsets):
    channels, length_a = series_a.shape
    length_b = series_b.shape[1]
    count = rows * cols
    share_a = NA // cols
    share_b = NB // rows
    vmem = pl.BlockSpec(memory_space=pltpu.VMEM)
    hbm = pl.BlockSpec(memory_space=pltpu.HBM)
    dma = pltpu.SemaphoreType.DMA
    f32 = jnp.float32
    a_best, b_best = pl.pallas_call(
        functools.partial(kernel, rows, cols),
        out_shape=(
            pltpu.VMEM((K, share_a), f32),
            pltpu.VMEM((K, share_b), f32),
        ),
        in_specs=[hbm] * 4,
        out_specs=(vmem, vmem),
        scratch_shapes=[
            pltpu.SMEM((1,), jnp.int32),
            pltpu.SMEM((1,), jnp.int32),
            pltpu.VMEM((SUB, LANES), jnp.int32),
            pltpu.VMEM((SUB, LANES), jnp.int32),
            pltpu.VMEM((6, channels, length_a), f32),
            pltpu.VMEM((count, channels, length_b), f32),
            pltpu.VMEM((2, channels, LANES, WIDE), f32),
            pltpu.VMEM((channels, LANES, WIDE), f32),
            pltpu.VMEM((2, NA, channels * M), jnp.bfloat16),
            pltpu.VMEM((channels * M, NB), jnp.bfloat16),
            pltpu.VMEM((2, NA, 2 * channels * LANES), f32),
            pltpu.VMEM((NA, NB), f32),
            pltpu.VMEM((NA, NB // 2), f32),
            pltpu.VMEM((NB, NA), f32),
            pltpu.VMEM((cols, K, share_a), f32),
            pltpu.VMEM((rows // 2, K * share_b // LANES, LANES), f32),
            pltpu.VMEM((cols, K, share_a), f32),
            pltpu.VMEM((rows // 2, K * share_b // LANES, LANES), f32),
            dma((4,)),
            dma((1,)),
            dma((1,)),
            dma((6,)),
            dma((6,)),
            dma((count,)),
            dma((count,)),
            dma((cols,)),
            dma((cols,)),
            dma((rows // 2,)),
            dma((rows // 2,)),
        ],
        compiler_params=pltpu.CompilerParams(collective_id=0, has_side_effects=True),
        name="join",
    )(a_offsets, b_offsets, series_a, series_b)
    return (a_best.T, b_best.T[None])


def solution(mesh):
    in_specs = (
        P(None, ("groups", "rows")),
        P(None, ("groups", "rows", "cols")),
        P(("groups", "rows")),
        P(("groups", "cols")),
    )
    out_specs = (P(("groups", "rows", "cols"), None), P(("groups", "cols"), "rows", None))
    body = functools.partial(local, mesh.shape["rows"], mesh.shape["cols"])
    return jax.shard_map(body, mesh=mesh, in_specs=in_specs, out_specs=out_specs, check_vma=False)
```

time: 22.8 us -> 24 us (1.053)
  Pallas kernels: 19.5 us -> 20.7 us
    pallas_call x1, Pallas kernels: 19.5 us -> 20.7 us  [local(): pl.pallas_call(functools.partial(kernel, rows, cols), out_shape=(pltpu.VM...]
where the time goes in v1:
time: 24 us; the launch traced here: 23.8 us
  Pallas kernels  20.7 us (86%)
  between operations  1.93 us (8%)
  local copies, waits for them, and re-layouts  1.21 us (5%)
    pallas_call x1, Pallas kernels, local(): pl.pallas_call(functools.partial(kernel, rows, cols), out_shape=(pltpu.VM...  20.7 us
    unnamed x2, local copies, waits for them, and re-layouts  1.21 us

profile of v1, /device:TPU:0, one launch (start us, length us, event | category | flops | bytes accessed | tf_op | source)
XLA Modules:
  0.0 23.8 jit_solution(9528662532966251737)
XLA Ops:
  1.9 20.7 %join.1 = (f32[16,256]{1,0:T(8,128)S(1)}, f32[16,64]{1,0:T(8,128)S(1)}) custom-call(s32[1]{0:T(128)S(6)} %copy.10.aoff_hbm, s32[1]{0:T(128)S(6)} %copy.11.boff_hbm, f32[4,512]{1,0:T(4,128)} %a_hbm.1, f32[4,64]{1,0:T(4,128)} %b_hbm.1), custom_call_target="tpu_custom_call" | custom-call | tf_op jit(solution)/shard_map/join/pallas_call | solution.py:312
  22.6 0.6 %copy.8 = f32[256,16]{0,1:T(8,128)} copy(f32[256,16]{0,1:T(8,128)S(1)} %bitcast.4) | data formatting | bytes 32768
  23.2 0.6 %copy.9 = f32[1,64,16]{1,2,0:T(8,128)} copy(f32[1,64,16]{1,2,0:T(8,128)S(1)} %bitcast.5) | data formatting | bytes 8192

commit v2 on v0

--- a/solution.py
+++ b/solution.py
@@ -73,48 +73,54 @@
     return merge_sublanes(lists)
 
 
-def hankel(segment, h_ref):
-    sums = []
-    sub = lax.broadcasted_iota(jnp.int32, (SUB, SPAN), 0)
-    for c in range(segment.shape[0]):
-        t = jnp.broadcast_to(segment[c : c + 1], (SUB, SPAN))
-        for bit in (1, 2, 4):
-            t = jnp.where((sub & bit) != 0, pltpu.roll(t, SPAN - bit, 1), t)
-        total = None
-        for b in range(LANES // SUB):
-            piece = t if b == 0 else pltpu.roll(t, SPAN - SUB * b, 1)
-            piece = piece[:, :WIDE]
-            h_ref[c, SUB * b : SUB * b + SUB, :] = piece
-            total = piece if total is None else total + piece
-        sums.append(jnp.sum(total, axis=0, keepdims=True))
-    return sums
-
-
-def unit_stats(h_ref, sums):
-    found = []
-    parts = range(M // LANES)
-    for c in range(len(sums)):
-        centre = sums[c] * (1.0 / LANES)
-        about = jnp.broadcast_to(centre, (SUB, WIDE))
-
-        def squares(b, total):
-            d = h_ref[c, pl.ds(pl.multiple_of(b * SUB, SUB), SUB), :] - about
-            return total + d * d
-
-        total = lax.fori_loop(0, LANES // SUB, squares, jnp.zeros((SUB, WIDE), jnp.float32), unroll=16)
-        within = jnp.sum(total, axis=0, keepdims=True)
-        means = [centre[:, LANES * q : LANES * q + NA] for q in parts]
-        mean = sum(means[1:], means[0]) * (LANES / M)
-        spread = sum(within[:, LANES * q : LANES * q + NA] for q in parts)
-        for v in means:
-            spread = spread + LANES * ((v - mean) * (v - mean))
-        found.append((mean, lax.rsqrt(spread * (1.0 / M) + 1e-05)))
-    return found
+def octets(segments, base_ref):
+    for s in range(SUB):
+        moved = segments if s == 0 else pltpu.roll(segments, SPAN - s, 1)
+        for t in range(SPAN // LANES):
+            base_ref[t, pl.ds(s, segments.shape[0], stride=SUB), :] = moved[:, LANES * t : LANES * t + LANES]
+
+
+def hankel(base_ref, h_ref, c):
+    rows = pl.ds(SUB * c, SUB)
+    t = jnp.concatenate([base_ref[v, rows, :] for v in range(SPAN // LANES)], axis=1)
+    for b in range(LANES // SUB):
+        piece = t if b == 0 else pltpu.roll(t, SPAN - SUB * b, 1)
+        h_ref[c, SUB * b : SUB * b + SUB, :] = piece[:, :WIDE]
+
+
+def window_stats(segment):
+    mean, squares, n = segment, None, 1
+    step = M // 2
+    while step >= 1:
+        width = mean.shape[1]
+
+        def pair(v):
+            if step >= LANES:
+                return v[:, : width - step], v[:, step:]
+            return v, pltpu.roll(v, width - step, 1)
+
+        a, b = pair(mean)
+        gap = b - a
+        mean = (a + b) * 0.5
+        between = gap * gap * (0.5 * n)
+        if squares is None:
+            squares = between
+        else:
+            a, b = pair(squares)
+            squares = (a + b) + between
+        n *= 2
+        step = step // 2
+    return mean[:, :NA], lax.rsqrt(squares[:, :NA] * (1.0 / M) + 1e-05)
+
+
+def shifted(x, lanes):
+    lanes %= x.shape[1]
+    return x if lanes == 0 else pltpu.roll(x, lanes, 1)
 
 
 def kernel(
     rows, cols, aoff_hbm, boff_hbm, a_hbm, b_hbm, a_out, b_out,
-    aoff, boff, abuf, bbuf, ha, hb, left, right, spread_out, score, score_t, alist, blist, arecv, brecv,
+    aoff, boff, abuf, bbuf, base, ha, left, right, spread_out, score, score_t, alist, blist, arecv, brecv,
     own_sem, a_send, a_recv, b_send, b_recv, la_send, la_recv, lb_send, lb_recv,
 ):
     channels = a_hbm.shape[0]
@@ -128,9 +134,12 @@
         y = x + d
         return y if d == 0 else jnp.where(y >= n, y - n, y)
 
-    along = [ahead(r, d, rows) for d in range(rows)]
+    if rows & (rows - 1):
+        along = [ahead(r, d, rows) for d in range(rows)]
+    else:
+        along = [r ^ d for d in range(rows)]
     across = [ahead(k, d, cols) for d in range(cols)]
-    peers = [(i, j) for i in along for j in across][1:]
+    peers = [(i, j) for i in along[::-1] for j in across[::-1]][:-1]
 
     own_a = pltpu.make_async_copy(a_hbm, abuf.at[1], own_sem.at[0])
     own_b = pltpu.make_async_copy(b_hbm, bbuf.at[me], own_sem.at[1])
@@ -144,8 +153,8 @@
         pl.semaphore_signal(barrier, inc=1, device_id=(g, i, j), device_id_type=MESH)
     pl.semaphore_wait(barrier, count - 1)
 
-    after = along[1]
-    before = along[rows - 1]
+    after = ahead(r, 1, rows)
+    before = ahead(r, rows - 1, rows)
     a_copies = [
         pltpu.make_async_remote_copy(
             src_ref=a_hbm, dst_ref=abuf.at[slot], send_sem=a_send.at[slot], recv_sem=a_recv.at[slot],
@@ -165,15 +174,28 @@
         )
         b_copies[-1].start()
 
-    own_a.wait()
-    offset_a.wait()
+    for copy in (own_a, offset_a, own_b, offset_b):
+        copy.wait()
     for copy in a_copies:
         copy.wait_recv()
+    for d, (i, j) in enumerate(peers):
+        source = i * cols + j
+        pltpu.make_async_remote_copy(
+            src_ref=b_hbm, dst_ref=bbuf.at[source], send_sem=b_send.at[d], recv_sem=b_recv.at[source],
+            device_id=(g, i, j), device_id_type=MESH,
+        ).wait_recv()
     padded = jnp.concatenate([abuf[0], abuf[1], abuf[2]], axis=1)
     extent = padded.shape[1]
     segment = pltpu.roll(padded, lax.rem(extent - aoff[0], extent), 1)[:, :SPAN]
-    stats = unit_stats(ha, hankel(segment, ha))
-    rest = jnp.concatenate([v for pair in stats for v in pair], axis=0)
+    whole = jnp.concatenate([bbuf[p] for p in range(count)], axis=1)
+    extent_b = whole.shape[1]
+    start = lax.rem(k * NB + boff[0], extent_b)
+    segment_b = pltpu.roll(whole, lax.rem(extent_b - start, extent_b), 1)[:, :SPAN]
+    segments = jnp.concatenate([segment, segment_b], axis=0)
+    octets(segments, base)
+    means, scales = window_stats(segments)
+
+    rest = jnp.concatenate([means[:channels], scales[:channels]], axis=0)
     pieces = []
     for _ in range(3):
         pieces.append(rest.astype(jnp.bfloat16).astype(jnp.float32))
@@ -186,49 +208,32 @@
         split, jnp.where(chosen, 1.0, 0.0).astype(jnp.bfloat16), preferred_element_type=jnp.float32
     )
 
-    @pl.loop(0, LANES // 16, unroll=True)
-    def _(b):
-        at = pl.multiple_of(b * 16, 16)
-        for q in range(NA // LANES):
-            row = pl.multiple_of(at + LANES * q, 16)
-            for c in range(channels):
-                mean = spread_out[pl.ds(row, 16), 2 * c * LANES : (2 * c + 1) * LANES]
-                scale = spread_out[pl.ds(row, 16), (2 * c + 1) * LANES : (2 * c + 2) * LANES]
+    for c in range(channels):
+        hankel(base, ha, c)
+        hankel(base, ha, channels + c)
+        for at in range(0, LANES, 16):
+            for q in range(NA // LANES):
+                row = at + LANES * q
+                mean = spread_out[row : row + 16, c * LANES : (c + 1) * LANES]
+                scale = spread_out[row : row + 16, (channels + c) * LANES : (channels + c + 1) * LANES]
                 for m in range(0, M, LANES):
-                    w = ha[c, pl.ds(at, 16), LANES * q + m : LANES * q + m + LANES]
-                    left[pl.ds(row, 16), M * c + m : M * c + m + LANES] = ((w - mean) * scale).astype(jnp.bfloat16)
-
-    own_b.wait()
-    offset_b.wait()
-    for d, (i, j) in enumerate(peers):
-        source = i * cols + j
-        pltpu.make_async_remote_copy(
-            src_ref=b_hbm, dst_ref=bbuf.at[source], send_sem=b_send.at[d], recv_sem=b_recv.at[source],
-            device_id=(g, i, j), device_id_type=MESH,
-        ).wait_recv()
-    whole = jnp.concatenate([bbuf[p] for p in range(count)], axis=1)
-    extent_b = whole.shape[1]
-    start = lax.rem(k * NB + boff[0], extent_b)
-    segment_b = pltpu.roll(whole, lax.rem(extent_b - start, extent_b), 1)
-    stats_b = unit_stats(hb, hankel(segment_b, hb))
-    for c in range(channels):
-        mean16 = jnp.broadcast_to(stats_b[c][0], (16, NB))
-        scale16 = jnp.broadcast_to(stats_b[c][1], (16, NB))
-
-        @pl.loop(0, LANES // 16, unroll=True)
-        def _(b):
-            at = pl.multiple_of(b * 16, 16)
+                    w = ha[c, at : at + 16, LANES * q + m : LANES * q + m + LANES]
+                    left[row : row + 16, M * c + m : M * c + m + LANES] = ((w - mean) * scale).astype(jnp.bfloat16)
+        mean16 = jnp.broadcast_to(means[channels + c : channels + c + 1], (16, NB))
+        scale16 = jnp.broadcast_to(scales[channels + c : channels + c + 1], (16, NB))
+        for at in range(0, LANES, 16):
             for q in range(M // LANES):
-                w = hb[c, pl.ds(at, 16), LANES * q : LANES * q + NB]
-                right[pl.ds(pl.multiple_of(at + M * c + LANES * q, 16), 16), :] = (
-                    (w - mean16) * scale16
-                ).astype(jnp.bfloat16)
+                w = ha[channels + c, at : at + 16, LANES * q : LANES * q + NB]
+                row = at + M * c + LANES * q
+                right[row : row + 16, :] = ((w - mean16) * scale16).astype(jnp.bfloat16)
 
     score[...] = jnp.dot(left[...], right[...], preferred_element_type=jnp.float32) * (1.0 / (channels * M))
 
     share_b = NB // rows
     per = LANES // share_b
     tiles = NB // LANES
+    depth = K // per
+    block = lax.broadcasted_iota(jnp.int32, (depth, LANES), 1) // share_b
     own = r // per
     place = r - own * per
     lb_copies = []
@@ -254,7 +259,11 @@
             )
         found = jnp.concatenate(top_columns(score, pl.ds(pl.multiple_of(LANES * t, LANES), LANES)), axis=0)
         for u in range(per):
-            blist[t * per + u] = found[:, u * share_b : (u + 1) * share_b]
+            packed = None
+            for v in range(per):
+                piece = shifted(found[depth * v : depth * v + depth], (v - u) * share_b)
+                packed = piece if packed is None else jnp.where(block == v, piece, packed)
+            blist[t * per + u] = packed
         for u in range(per - 1 if n == tiles - 1 else per):
             send_list(t * per + (ahead(place, u + 1, per) if n == tiles - 1 else u))
     brecv[r] = blist[r]
@@ -276,12 +285,12 @@
         la_copies[-1].start()
 
     for d in range(1, rows):
-        source = along[d]
+        source = ahead(r, d, rows)
         pltpu.make_async_remote_copy(
             src_ref=blist.at[source], dst_ref=brecv.at[source], send_sem=lb_send.at[d], recv_sem=lb_recv.at[source],
             device_id=(g, source, k), device_id_type=MESH,
         ).wait_recv()
-    lists = [brecv[:, j, :] for j in range(K)]
+    lists = [brecv[:, j % depth, (j // depth) * share_b : (j // depth + 1) * share_b] for j in range(K)]
     b_out[...] = jnp.concatenate(merge_sublanes(lists), axis=0)
 
     held = alist[k]
@@ -323,17 +332,17 @@
             pltpu.SMEM((1,), jnp.int32),
             pltpu.VMEM((3, channels, length_a), f32),
             pltpu.VMEM((count, channels, length_b), f32),
-            pltpu.VMEM((channels, LANES, WIDE), f32),
-            pltpu.VMEM((channels, LANES, WIDE), f32),
+            pltpu.VMEM((SPAN // LANES, 2 * channels * SUB, LANES), f32),
+            pltpu.VMEM((2 * channels, LANES, WIDE), f32),
             pltpu.VMEM((NA, channels * M), jnp.bfloat16),
             pltpu.VMEM((channels * M, NB), jnp.bfloat16),
             pltpu.VMEM((NA, 2 * channels * LANES), f32),
             pltpu.VMEM((NA, NB), f32),
             pltpu.VMEM((NB, NA), f32),
             pltpu.VMEM((cols, K, share_a), f32),
-            pltpu.VMEM((rows, K, share_b), f32),
+            pltpu.VMEM((rows, K * share_b // LANES, LANES), f32),
             pltpu.VMEM((cols, K, share_a), f32),
-            pltpu.VMEM((rows, K, share_b), f32),
+            pltpu.VMEM((rows, K * share_b // LANES, LANES), f32),
             dma((4,)),
             dma((3,)),
             dma((3,)),

time: 22.8 us -> 21.2 us (0.930)
  Pallas kernels: 19.5 us -> 17.9 us
    pallas_call x1, Pallas kernels: 19.5 us -> 17.9 us  [local(): pl.pallas_call(functools.partial(kernel, rows, cols), out_shape=(pltpu.VM...]
where the time goes in v2:
time: 21.2 us; the launch traced here: 21 us
  Pallas kernels  17.9 us (84%)
  between operations  1.93 us (9%)
  local copies, waits for them, and re-layouts  1.21 us (6%)
    pallas_call x1, Pallas kernels, local(): pl.pallas_call(functools.partial(kernel, rows, cols), out_shape=(pltpu.VM...  17.9 us
    unnamed x2, local copies, waits for them, and re-layouts  1.21 us

profile of v2, /device:TPU:0, one launch (start us, length us, event | category | flops | bytes accessed | tf_op | source)
XLA Modules:
  0.0 21.0 jit_solution(11041501839000183084)
XLA Ops:
  1.9 17.9 %join.1 = (f32[16,256]{1,0:T(8,128)S(1)}, f32[16,64]{1,0:T(8,128)S(1)}) custom-call(s32[1]{0:T(128)S(6)} %copy.10.aoff_hbm, s32[1]{0:T(128)S(6)} %copy.11.boff_hbm, f32[4,512]{1,0:T(4,128)} %a_hbm.1, f32[4,64]{1,0:T(4,128)} %b_hbm.1), custom_call_target="tpu_custom_call" | custom-call | tf_op jit(solution)/shard_map/join/pallas_call | solution.py:322
  19.8 0.6 %copy.8 = f32[256,16]{0,1:T(8,128)} copy(f32[256,16]{0,1:T(8,128)S(1)} %bitcast.4) | data formatting | bytes 32768
  20.4 0.6 %copy.9 = f32[1,64,16]{1,2,0:T(8,128)} copy(f32[1,64,16]{1,2,0:T(8,128)S(1)} %bitcast.5) | data formatting | bytes 8192

commit v3 on v2

--- a/solution.py
+++ b/solution.py
@@ -193,6 +193,8 @@
     segment_b = pltpu.roll(whole, lax.rem(extent_b - start, extent_b), 1)[:, :SPAN]
     segments = jnp.concatenate([segment, segment_b], axis=0)
     octets(segments, base)
+    hankel(base, ha, 0)
+    hankel(base, ha, channels)
     means, scales = window_stats(segments)
 
     rest = jnp.concatenate([means[:channels], scales[:channels]], axis=0)
@@ -209,8 +211,9 @@
     )
 
     for c in range(channels):
-        hankel(base, ha, c)
-        hankel(base, ha, channels + c)
+        if c + 1 < channels:
+            hankel(base, ha, c + 1)
+            hankel(base, ha, channels + c + 1)
         for at in range(0, LANES, 16):
             for q in range(NA // LANES):
                 row = at + LANES * q
@@ -284,15 +287,6 @@
         )
         la_copies[-1].start()
 
-    for d in range(1, rows):
-        source = ahead(r, d, rows)
-        pltpu.make_async_remote_copy(
-            src_ref=blist.at[source], dst_ref=brecv.at[source], send_sem=lb_send.at[d], recv_sem=lb_recv.at[source],
-            device_id=(g, source, k), device_id_type=MESH,
-        ).wait_recv()
-    lists = [brecv[:, j % depth, (j // depth) * share_b : (j // depth + 1) * share_b] for j in range(K)]
-    b_out[...] = jnp.concatenate(merge_sublanes(lists), axis=0)
-
     held = alist[k]
     best = [held[j : j + 1] for j in range(K)]
     for d in range(1, cols):
@@ -304,6 +298,15 @@
         came = arecv[source]
         best = merge_top(best, [came[j : j + 1] for j in range(K)])
     a_out[...] = jnp.concatenate(best, axis=0)
+
+    for d in range(1, rows):
+        source = ahead(r, d, rows)
+        pltpu.make_async_remote_copy(
+            src_ref=blist.at[source], dst_ref=brecv.at[source], send_sem=lb_send.at[d], recv_sem=lb_recv.at[source],
+            device_id=(g, source, k), device_id_type=MESH,
+        ).wait_recv()
+    lists = [brecv[:, j % depth, (j // depth) * share_b : (j // depth + 1) * share_b] for j in range(K)]
+    b_out[...] = jnp.concatenate(merge_sublanes(lists), axis=0)
 
     for copy in a_copies + b_copies + lb_copies + la_copies:
         copy.wait_send()

time: 21.2 us -> 21.1 us (level)
  no operation moved by 1% of the time
where the time goes in v3:
time: 21.1 us; the launch traced here: 21 us
  Pallas kernels  17.8 us (84%)
  between operations  1.93 us (9%)
  local copies, waits for them, and re-layouts  1.21 us (6%)
    pallas_call x1, Pallas kernels, local(): pl.pallas_call(functools.partial(kernel, rows, cols), out_shape=(pltpu.VM...  17.8 us
    unnamed x2, local copies, waits for them, and re-layouts  1.21 us

profile of v3, /device:TPU:0, one launch (start us, length us, event | category | flops | bytes accessed | tf_op | source)
XLA Modules:
  0.0 21.0 jit_solution(3817198455757709509)
XLA Ops:
  1.9 17.8 %join.1 = (f32[16,256]{1,0:T(8,128)S(1)}, f32[16,64]{1,0:T(8,128)S(1)}) custom-call(s32[1]{0:T(128)S(6)} %copy.10.aoff_hbm, s32[1]{0:T(128)S(6)} %copy.11.boff_hbm, f32[4,512]{1,0:T(4,128)} %a_hbm.1, f32[4,64]{1,0:T(4,128)} %b_hbm.1), custom_call_target="tpu_custom_call" | custom-call | tf_op jit(solution)/shard_map/join/pallas_call | solution.py:325
  19.8 0.6 %copy.8 = f32[256,16]{0,1:T(8,128)} copy(f32[256,16]{0,1:T(8,128)S(1)} %bitcast.4) | data formatting | bytes 32768
  20.4 0.6 %copy.9 = f32[1,64,16]{1,2,0:T(8,128)} copy(f32[1,64,16]{1,2,0:T(8,128)S(1)} %bitcast.5) | data formatting | bytes 8192

commit v4 on v3

--- a/solution.py
+++ b/solution.py
@@ -141,6 +141,9 @@
     across = [ahead(k, d, cols) for d in range(cols)]
     peers = [(i, j) for i in along[::-1] for j in across[::-1]][:-1]
 
+    barrier = pltpu.get_barrier_semaphore()
+    for i, j in peers:
+        pl.semaphore_signal(barrier, inc=1, device_id=(g, i, j), device_id_type=MESH)
     own_a = pltpu.make_async_copy(a_hbm, abuf.at[1], own_sem.at[0])
     own_b = pltpu.make_async_copy(b_hbm, bbuf.at[me], own_sem.at[1])
     offset_a = pltpu.make_async_copy(aoff_hbm, aoff, own_sem.at[2])
@@ -148,9 +151,6 @@
     for copy in (own_a, own_b, offset_a, offset_b):
         copy.start()
 
-    barrier = pltpu.get_barrier_semaphore()
-    for i, j in peers:
-        pl.semaphore_signal(barrier, inc=1, device_id=(g, i, j), device_id_type=MESH)
     pl.semaphore_wait(barrier, count - 1)
 
     after = ahead(r, 1, rows)
@@ -193,8 +193,6 @@
     segment_b = pltpu.roll(whole, lax.rem(extent_b - start, extent_b), 1)[:, :SPAN]
     segments = jnp.concatenate([segment, segment_b], axis=0)
     octets(segments, base)
-    hankel(base, ha, 0)
-    hankel(base, ha, channels)
     means, scales = window_stats(segments)
 
     rest = jnp.concatenate([means[:channels], scales[:channels]], axis=0)
@@ -204,21 +202,20 @@
         rest = rest - pieces[-1]
     split = jnp.concatenate(pieces, axis=0).T.astype(jnp.bfloat16)
     kinds = 2 * channels
-    shape = (3 * kinds, kinds * LANES)
-    chosen = lax.broadcasted_iota(jnp.int32, shape, 0) % kinds == lax.broadcasted_iota(jnp.int32, shape, 1) // LANES
-    spread_out[...] = jnp.dot(
-        split, jnp.where(chosen, 1.0, 0.0).astype(jnp.bfloat16), preferred_element_type=jnp.float32
-    )
+    shape = (3 * kinds, 2 * LANES)
+    kind = lax.broadcasted_iota(jnp.int32, shape, 0) % kinds
+    wanted = lax.broadcasted_iota(jnp.int32, shape, 1) // LANES * channels
 
     for c in range(channels):
-        if c + 1 < channels:
-            hankel(base, ha, c + 1)
-            hankel(base, ha, channels + c + 1)
+        hankel(base, ha, c)
+        hankel(base, ha, channels + c)
+        chosen = jnp.where(kind == wanted + c, 1.0, 0.0).astype(jnp.bfloat16)
+        spread_out[c] = jnp.dot(split, chosen, preferred_element_type=jnp.float32)
         for at in range(0, LANES, 16):
             for q in range(NA // LANES):
                 row = at + LANES * q
-                mean = spread_out[row : row + 16, c * LANES : (c + 1) * LANES]
-                scale = spread_out[row : row + 16, (channels + c) * LANES : (channels + c + 1) * LANES]
+                mean = spread_out[c, row : row + 16, :LANES]
+                scale = spread_out[c, row : row + 16, LANES:]
                 for m in range(0, M, LANES):
                     w = ha[c, at : at + 16, LANES * q + m : LANES * q + m + LANES]
                     left[row : row + 16, M * c + m : M * c + m + LANES] = ((w - mean) * scale).astype(jnp.bfloat16)
@@ -230,7 +227,8 @@
                 row = at + M * c + LANES * q
                 right[row : row + 16, :] = ((w - mean16) * scale16).astype(jnp.bfloat16)
 
-    score[...] = jnp.dot(left[...], right[...], preferred_element_type=jnp.float32) * (1.0 / (channels * M))
+    score[...] = jnp.dot(left[...], right[...], preferred_element_type=jnp.float32)
+    factor = 1.0 / (channels * M)
 
     share_b = NB // rows
     per = LANES // share_b
@@ -297,7 +295,7 @@
         ).wait_recv()
         came = arecv[source]
         best = merge_top(best, [came[j : j + 1] for j in range(K)])
-    a_out[...] = jnp.concatenate(best, axis=0)
+    a_out[...] = jnp.concatenate(best, axis=0) * factor
 
     for d in range(1, rows):
         source = ahead(r, d, rows)
@@ -306,7 +304,7 @@
             device_id=(g, source, k), device_id_type=MESH,
         ).wait_recv()
     lists = [brecv[:, j % depth, (j // depth) * share_b : (j // depth + 1) * share_b] for j in range(K)]
-    b_out[...] = jnp.concatenate(merge_sublanes(lists), axis=0)
+    b_out[...] = jnp.concatenate(merge_sublanes(lists), axis=0) * factor
 
     for copy in a_copies + b_copies + lb_copies + la_copies:
         copy.wait_send()
@@ -339,7 +337,7 @@
             pltpu.VMEM((2 * channels, LANES, WIDE), f32),
             pltpu.VMEM((NA, channels * M), jnp.bfloat16),
             pltpu.VMEM((channels * M, NB), jnp.bfloat16),
-            pltpu.VMEM((NA, 2 * channels * LANES), f32),
+            pltpu.VMEM((channels, NA, 2 * LANES), f32),
             pltpu.VMEM((NA, NB), f32),
             pltpu.VMEM((NB, NA), f32),
             pltpu.VMEM((cols, K, share_a), f32),

time: 21.1 us -> 21.1 us (level)
  no operation moved by 1% of the time
where the time goes in v4:
time: 21.1 us; the launch traced here: 21 us
  Pallas kernels  17.8 us (84%)
  between operations  1.93 us (9%)
  local copies, waits for them, and re-layouts  1.21 us (6%)
    pallas_call x1, Pallas kernels, local(): pl.pallas_call(functools.partial(kernel, rows, cols), out_shape=(pltpu.VM...  17.8 us
    unnamed x2, local copies, waits for them, and re-layouts  1.21 us

profile of v4, /device:TPU:0, one launch (start us, length us, event | category | flops | bytes accessed | tf_op | source)
XLA Modules:
  0.0 21.0 jit_solution(7411954305046224928)
XLA Ops:
  1.9 17.8 %join.1 = (f32[16,256]{1,0:T(8,128)S(1)}, f32[16,64]{1,0:T(8,128)S(1)}) custom-call(s32[1]{0:T(128)S(6)} %copy.10.aoff_hbm, s32[1]{0:T(128)S(6)} %copy.11.boff_hbm, f32[4,512]{1,0:T(4,128)} %a_hbm.1, f32[4,64]{1,0:T(4,128)} %b_hbm.1), custom_call_target="tpu_custom_call" | custom-call | tf_op jit(solution)/shard_map/join/pallas_call | solution.py:323
  19.8 0.6 %copy.8 = f32[256,16]{0,1:T(8,128)} copy(f32[256,16]{0,1:T(8,128)S(1)} %bitcast.4) | data formatting | bytes 32768
  20.4 0.6 %copy.9 = f32[1,64,16]{1,2,0:T(8,128)} copy(f32[1,64,16]{1,2,0:T(8,128)S(1)} %bitcast.5) | data formatting | bytes 8192
